TPU v7x, 256 devices: a whole 4x4x8 slice. The times are simulated.
256 devices in a mesh: dp: 16 (over z_hi, y, core), expert: 16 (over x, z_lo).
Axes of the slice: x: 4, y: 4, z: 8 (z_hi: 2, z_lo: 4; z = z_hi * 4 + z_lo), core: 2. Of those that a mesh axis runs over, the one named last changes fastest.
Arguments:
- images: bfloat16 [1024, 256, 1280], P(('dp', 'expert')), may hold values from -16 to 16
- router: bfloat16 [1280, 128], replicated, as said below
- w_in: bfloat16 [256, 1280, 1280], P(('dp', 'expert')), may hold values from -0.15625 to 0.15625
- w_out: bfloat16 [256, 1280, 1280], P(('dp', 'expert')), may hold values from -0.125 to 0.125
- keep_bits: int32 [1024, 256, 128], P(None, ('dp', 'expert')), may hold values from 0 to 1023, as said below
Outputs:
- mixed: bfloat16 [1024, 256, 1280], P(('dp', 'expert'))
Inputs may be any that keep to these rules, and one draw needn't show every extreme that they name: `router`: each entry within 18 / sqrt(1280) in magnitude. `keep_bits`: bit i of word w stands for hidden unit 10 * w + i.
All inputs are finite; a program needn't handle non-finite values.
Results may differ from a plain program's by a relative error of at most 0.017.
Values may be sent and summed in bfloat16 or wider, within the bound.
A program may use at most 128 MiB of HBM per device.

v0:
```python
import jax
import jax.numpy as jnp
from jax import lax
from jax.sharding import PartitionSpec as P

SPLIT = 2
keep_rate = 0.875


def unpack_flags(words):
    shifts = jnp.arange(10, dtype=jnp.int32)
    flags = jnp.right_shift(words[..., None], shifts) & 1
    return flags.reshape(words.shape[:-1] + (words.shape[-1] * 10,)).astype(jnp.float32)


def expert_piece(slot_rows, w_in, w_out, kept_units):
    pre_act = jnp.dot(slot_rows, w_in[0], preferred_element_type=jnp.float32)
    hidden = (jax.nn.gelu(pre_act) * kept_units * (1.0 / keep_rate)).astype(jnp.bfloat16)
    return jnp.dot(hidden, w_out[0], preferred_element_type=jnp.float32).astype(jnp.bfloat16)


def on_device(images, router, w_in, w_out, keep_bits):
    image_count = images.shape[0]
    width = images.shape[2]
    experts = router.shape[1]
    dp_count = lax.axis_size("dp")
    expert_count = lax.axis_size("expert")
    logits = jnp.einsum("bmd,de->bme", images, router, preferred_element_type=jnp.float32)
    dispatch = jax.nn.softmax(logits, axis=1).astype(jnp.bfloat16)
    combine = jax.nn.softmax(logits, axis=2).astype(jnp.bfloat16)
    slot_values = jnp.einsum(
        "bme,bmd->bed", dispatch, images, preferred_element_type=jnp.float32
    ).astype(jnp.bfloat16)
    kept_units = unpack_flags(keep_bits[:, 0, :])
    doubled = jnp.repeat(slot_values, SPLIT, axis=1).reshape(
        image_count, dp_count, expert_count, width
    )
    across = lax.all_to_all(doubled, "expert", split_axis=2, concat_axis=0, tiled=True)
    arrived = lax.all_to_all(across, "dp", split_axis=1, concat_axis=0, tiled=True)
    partial_value = expert_piece(arrived.reshape(-1, width), w_in, w_out, kept_units)
    returned = lax.all_to_all(
        partial_value.reshape(-1, 1, 1, width), "dp", split_axis=0, concat_axis=1, tiled=True
    )
    returned = lax.all_to_all(returned, "expert", split_axis=0, concat_axis=2, tiled=True)
    paired = returned.reshape(image_count, experts, SPLIT, width)
    expert_out = paired.astype(jnp.float32).sum(axis=2).astype(jnp.bfloat16)
    mixed = jnp.einsum("bme,bed->bmd", combine, expert_out, preferred_element_type=jnp.float32)
    return mixed.astype(jnp.bfloat16)


def solution(mesh):
    placed = (
        P(("dp", "expert"), None, None),
        P(),
        P(("dp", "expert"), None, None),
        P(("dp", "expert"), None, None),
        P(None, ("dp", "expert"), None),
    )
    return jax.shard_map(
        on_device,
        mesh=mesh,
        in_specs=placed,
        out_specs=P(("dp", "expert"), None, None),
        check_vma=False,
    )
```

profile of v0, /device:TPU:1, one launch (start us, length us, event | category | flops | bytes accessed | tf_op | source)
XLA Modules:
  0.0 342.5 jit_solution(12739725940960338433)
XLA Ops:
  0.0 2.7 fusion.27
  2.8 0.8 copy-done.2
  3.6 0.1 fusion.39
  3.7 3.7 %convolution_convert_fusion.2 = bf16[4,128,1280]{2,1,0:T(8,128)(2,1)} fusion(bf16[4,256,1280]{2,1,0:T(8,128)(2,1)} %param.5, f32[4,128]{1,0:T(4,128)S(1)} %fusion.39, f32[4,256,128]{2,1,0:T(8,128)} %copy-done.2), kind=kOutput, calls=%fused_computation.19 | convolution fusion | flops 336593664 | bytes 4458496 | tf_op jit(solution)/shard_map/bme,bmd->bed/dot_general | solution.py:31
  7.4 2.3 copy.31
  9.8 0.7 broadcast_in_dim.2
  10.5 1.2 copy.32
  11.7 69.5 %all_to_all.66 = bf16[4,16,16,1280]{3,0,1,2:T(4,128)(2,1)S(1)} all-to-all(bf16[4,16,16,1280]{3,0,1,2:T(4,128)(2,1)S(1)} %copy.32), channel_id=1, replica_groups=mesh['dp'=16,'expert'=16] {'expert'}, dimensions={2} | all-to-all | bytes 5242880 | tf_op jit(solution)/shard_map/all_to_all | solution.py:38
  81.2 0.4 copy.33
  81.6 2.3 copy.34
  83.9 10.1 %all-to-all-start.1 = ((bf16[64,16,1,1280]{3,0,2,1:T(8,128)(2,1)}), bf16[64,16,1,1280]{3,0,2,1:T(8,128)(2,1)}, u32[]{:S(2)}, u32[]{:S(2)}) async-start(bf16[64,16,1,1280]{3,0,2,1:T(8,128)(2,1)} %copy.34), calls=%async_computation.1 | async-start | bytes 5242880 | tf_op jit(solution)/shard_map/all_to_all | solution.py:39
  94.0 2.1 copy.37
  96.1 5.4 %shift_right_arithmetic.23 = s32[1024,128,10]{0,2,1:T(8,128)} broadcast(s32[1024,128]{0,1:T(8,128)} %copy.37), dimensions={0,1} | broadcast | bytes 5767168 | tf_op jit(solution)/shard_map/shift_right_arithmetic | solution.py:12
  101.5 7.9 %shift_right_arithmetic.24 = s32[1024,1280]{0,1:T(8,128)} reshape(s32[1024,128,10]{0,2,1:T(8,128)} %shift_right_arithmetic.23) | data formatting | bytes 10485760 | tf_op jit(solution)/shard_map/shift_right_arithmetic | solution.py:12
  109.4 5.9 %copy.38 = s32[1024,1280]{1,0:T(8,128)} copy(s32[1024,1280]{0,1:T(8,128)} %shift_right_arithmetic.24) | data formatting | bytes 10485760 | tf_op jit(solution)/shard_map/shift_right_arithmetic | solution.py:12
  115.5 41.3 %all-to-all-done.1 = bf16[64,16,1,1280]{3,0,2,1:T(8,128)(2,1)} async-done(((bf16[64,16,1,1280]{3,0,2,1:T(8,128)(2,1)}), bf16[64,16,1,1280]{3,0,2,1:T(8,128)(2,1)}, u32[]{:S(2)}, u32[]{:S(2)}) %all-to-all-start.1) | async-done | bytes 2621472 | tf_op jit(solution)/shard_map/all_to_all | solution.py:39
  156.8 3.2 copy.48
  159.9 2.3 copy.36
  162.2 11.8 %fusion.17 = bf16[1024,1,1,1280]{3,0,2,1:T(8,128)(2,1)} fusion(bf16[1,1280,1280]{2,1,0:T(8,128)(2,1)S(1)} %copy-done, s32[1024,1280]{1,0:T(8,128)} %copy.38, bf16[1024,1280]{1,0:T(8,128)(2,1)} %bitcast.54, bf16[1,1280,1280]{2,1,0:T(8,128)(2,1)} %param.7, s32[1280]{0:T(1024)S(1)} %shift_right_arithmetic.26), kind=kOutput, calls=%fused_computation.18 | convolution fusion | flops 6730547200 | bytes 17044480 | tf_op jit(solution)/shard_map/dot_general | solution.py:19
  174.0 0.5 broadcast.8
  174.6 4.5 %reduce.1 = bf16[1024,1280]{1,0:T(8,128)(2,1)S(1)} reduce(bf16[1024,1,1,1280]{3,0,2,1:T(8,128)(2,1)} %fusion.17, bf16[]{:T(256)} %broadcast.8), dimensions={1,2}, to_apply=%copy.39.reduce_sub_computation | reduce | bytes 5242882 | tf_op jit(solution)/shard_map/reshape | solution.py:42
  179.0 2.2 reshape.23
  181.2 57.8 %all_to_all.67 = bf16[16,2,40960]{2,1,0:T(2,128)(2,1)S(1)} all-to-all(bf16[16,2,40960]{2,1,0:T(2,128)(2,1)} %reshape.23), channel_id=1, replica_groups=mesh['dp'=16,'expert'=16] {'dp'}, dimensions={0} | all-to-all | bytes 5242880 | tf_op jit(solution)/shard_map/all_to_all | solution.py:41
  239.0 7.2 %reshape.24 = bf16[1024,1,1,1280]{3,2,1,0:T(2,128)(2,1)} reshape(bf16[16,2,40960]{2,1,0:T(2,128)(2,1)S(1)} %all_to_all.67) | data formatting | bytes 5242880
  246.2 2.9 copy.44
  249.1 2.9 copy.40
  252.0 15.0 %all-to-all-start.3 = ((bf16[64,16,1,1280]{3,1,2,0:T(8,128)(2,1)}), bf16[64,16,1,1280]{3,1,2,0:T(8,128)(2,1)S(1)}, u32[]{:S(2)}, u32[]{:S(2)}) async-start(bf16[64,16,1,1280]{3,1,2,0:T(8,128)(2,1)} %copy.40), calls=%async_computation.3 | async-start | bytes 5242880 | tf_op jit(solution)/shard_map/all_to_all | solution.py:44
  267.0 0.4 fusion.40
  267.4 61.9 %all-to-all-done.3 = bf16[64,16,1,1280]{3,1,2,0:T(8,128)(2,1)S(1)} async-done(((bf16[64,16,1,1280]{3,1,2,0:T(8,128)(2,1)}), bf16[64,16,1,1280]{3,1,2,0:T(8,128)(2,1)S(1)}, u32[]{:S(2)}, u32[]{:S(2)}) %all-to-all-start.3) | async-done | bytes 2621472 | tf_op jit(solution)/shard_map/all_to_all | solution.py:44
  329.3 2.8 copy.41
  332.1 5.1 %reduce_sum.32 = bf16[4,128,1280]{2,0,1:T(4,128)(2,1)} reduce(bf16[4,128,2,1280]{3,0,2,1:T(4,128)(2,1)} %bitcast.49, bf16[]{:T(256)} %constant.8.clone.1), dimensions={2}, to_apply=%region_4.0 | reduce | flops 655360 | bytes 3932162 | tf_op jit(solution)/shard_map/reduce_sum | solution.py:46
  337.2 5.3 %convolution_convert_fusion = bf16[4,256,1280]{2,1,0:T(8,128)(2,1)} fusion(bf16[4,128,1280]{2,0,1:T(4,128)(2,1)} %reduce_sum.32, f32[4,256]{1,0:T(4,128)S(1)} %fusion.40, f32[4,256,128]{2,1,0:T(8,128)} %copy-done.2), kind=kOutput, calls=%fused_computation.13 | convolution fusion | flops 337249408 | bytes 4460544 | tf_op jit(solution)/shard_map/bme,bed->bmd/dot_general | solution.py:47
  (9 shorter events, 0.2 us)
Async XLA Ops:
  0.0 162.2 %copy-start = (bf16[1,1280,1280]{2,1,0:T(8,128)(2,1)S(1)}, bf16[1,1280,1280]{2,1,0:T(8,128)(2,1)}, u32[]{:S(2)}) copy-start(bf16[1,1280,1280]{2,1,0:T(8,128)(2,1)} %param.8) | copy-start | bytes 9830404
  2.8 0.8 copy-start.2
  83.9 72.9 %all-to-all-start.1 = ((bf16[64,16,1,1280]{3,0,2,1:T(8,128)(2,1)}), bf16[64,16,1,1280]{3,0,2,1:T(8,128)(2,1)}, u32[]{:S(2)}, u32[]{:S(2)}) async-start(bf16[64,16,1,1280]{3,0,2,1:T(8,128)(2,1)} %copy.34), calls=%async_computation.1 | async-start | bytes 5242880 | tf_op jit(solution)/shard_map/all_to_all | solution.py:39
  252.0 15.0 %copy-start.3 = (f32[4,256,128]{2,1,0:T(8,128)S(1)}, f32[4,256,128]{2,1,0:T(8,128)}, u32[]{:S(2)}) copy-start(f32[4,256,128]{2,1,0:T(8,128)} %copy-done.2) | copy-start | bytes 1572868
  252.0 77.2 %all-to-all-start.3 = ((bf16[64,16,1,1280]{3,1,2,0:T(8,128)(2,1)}), bf16[64,16,1,1280]{3,1,2,0:T(8,128)(2,1)S(1)}, u32[]{:S(2)}, u32[]{:S(2)}) async-start(bf16[64,16,1,1280]{3,1,2,0:T(8,128)(2,1)} %copy.40), calls=%async_computation.3 | async-start | bytes 5242880 | tf_op jit(solution)/shard_map/all_to_all | solution.py:44
  332.1 10.4 %copy-start.1 = (bf16[1,1280,1280]{2,1,0:T(8,128)(2,1)S(1)}, bf16[1,1280,1280]{2,1,0:T(8,128)(2,1)}, u32[]{:S(2)}) copy-start(bf16[1,1280,1280]{2,1,0:T(8,128)(2,1)} %param.8) | copy-start | bytes 9830404
where the time goes:
time: 343 us; the launch traced here: 342 us
  blocking collectives  127 us (37%)
  waiting for transfers between devices  103 us (30%)
  local copies, waits for them, and re-layouts  53.2 us (16%)
  starting transfers between devices  25.1 us (7%)
  matrix products  23.6 us (7%)
  other arithmetic  10.1 us (3%)
    all_to_all x1, blocking collectives, on_device(): lax.all_to_all(doubled, 'expert', split_axis=2, concat_axis=0, tiled=True)  69.5 us
    all_to_all x1, waiting for transfers between devices, on_device(): lax.all_to_all(returned, 'expert', split_axis=0, concat_axis=2, tiled=True)  61.9 us
    all_to_all x1, blocking collectives, on_device(): lax.all_to_all(partial_value.reshape(-1, 1, 1, width), 'dp', split_axis=0...  57.8 us
    all_to_all x1, waiting for transfers between devices, on_device(): lax.all_to_all(across, 'dp', split_axis=1, concat_axis=0, tiled=True)  41.3 us
    shift_right_arithmetic x6, local copies, waits for them, and re-layouts, unpack_flags(): flags = jnp.right_shift(words[..., None], shifts) & 1  21.5 us
    all_to_all x1, starting transfers between devices, on_device(): lax.all_to_all(returned, 'expert', split_axis=0, concat_axis=2, tiled=True)  15 us
    unnamed x11, local copies, waits for them, and re-layouts  13.1 us
    dot_general x1, matrix products, expert_piece(): jnp.dot(hidden, w_out[0], preferred_element_type=jnp.float32)  11.8 us
  transfers between devices with their start and end apart: 2, of which 2 were waited for; matrix products, arithmetic and copies ran while one was open for 6% of the time, Pallas kernels for 0%

commit v1 on v0

--- a/solution.py
+++ b/solution.py
@@ -36,7 +36,10 @@
         image_count, dp_count, expert_count, width
     )
     across = lax.all_to_all(doubled, "expert", split_axis=2, concat_axis=0, tiled=True)
-    arrived = lax.all_to_all(across, "dp", split_axis=1, concat_axis=0, tiled=True)
+    arrived = jnp.concatenate(
+        lax.all_to_all(jnp.stack(jnp.split(across, lax.axis_size("dp"), axis=1)), "dp", 0, 0),
+        axis=0,
+    )
     partial_value = expert_piece(arrived.reshape(-1, width), w_in, w_out, kept_units)
     returned = lax.all_to_all(
         partial_value.reshape(-1, 1, 1, width), "dp", split_axis=0, concat_axis=1, tiled=True

time: 343 us -> 352 us (1.026)
  local copies, waits for them, and re-layouts: 53.2 us -> 62.2 us
    unnamed x11 -> x26, local copies, waits for them, and re-layouts: 13.1 us -> 23.4 us
    split x0 -> x1, local copies, waits for them, and re-layouts: none -> 5.71 us  [on_device(): jnp.split(across, lax.axis_size('dp'), axis=1)]
    all_to_all x2 -> x0, local copies, waits for them, and re-layouts: 5.45 us -> none  [on_device(): lax.all_to_all(across, 'dp', split_axis=1, concat_axis=0, tiled=True)]
where the time goes in v1:
time: 352 us
  blocking collectives  127 us (36%)
  waiting for transfers between devices  103 us (29%)
  local copies, waits for them, and re-layouts  62.2 us (18%)
  starting transfers between devices  25.1 us (7%)
  matrix products  23.6 us (7%)
  other arithmetic  10.1 us (3%)
    all_to_all x1, blocking collectives, on_device(): lax.all_to_all(doubled, 'expert', split_axis=2, concat_axis=0, tiled=True)  69.5 us
    all_to_all x1, waiting for transfers between devices, on_device(): lax.all_to_all(returned, 'expert', split_axis=0, concat_axis=2, tiled=True)  61.9 us
    all_to_all x1, blocking collectives, on_device(): lax.all_to_all(partial_value.reshape(-1, 1, 1, width), 'dp', split_axis=0...  57.8 us
    all_to_all x1, waiting for transfers between devices, on_device(): lax.all_to_all(jnp.stack(jnp.split(across, lax.axis_size('dp'), axis=1)),...  41.3 us
    unnamed x26, local copies, waits for them, and re-layouts  23.4 us
    shift_right_arithmetic x6, local copies, waits for them, and re-layouts, unpack_flags(): flags = jnp.right_shift(words[..., None], shifts) & 1  21.5 us
    all_to_all x1, starting transfers between devices, on_device(): lax.all_to_all(returned, 'expert', split_axis=0, concat_axis=2, tiled=True)  15 us
    dot_general x1, matrix products, expert_piece(): jnp.dot(hidden, w_out[0], preferred_element_type=jnp.float32)  11.8 us
  transfers between devices with their start and end apart: 2, of which 2 were waited for; matrix products, arithmetic and copies ran while one was open for 6% of the time, Pallas kernels for 0%

profile of v1, /device:TPU:1, one launch (start us, length us, event | category | flops | bytes accessed | tf_op | source)
XLA Modules:
  0.0 351.6 jit_solution(3386568633561916066)
XLA Ops:
  0.0 2.7 fusion.27
  2.8 0.8 copy-done.2
  3.7 3.7 %convolution_convert_fusion.2 = bf16[4,128,1280]{2,1,0:T(8,128)(2,1)} fusion(bf16[4,256,1280]{2,1,0:T(8,128)(2,1)} %param.5, f32[4,128]{1,0:T(4,128)S(1)} %fusion.40, f32[4,256,128]{2,1,0:T(8,128)} %copy-done.2), kind=kOutput, calls=%fused_computation.19 | convolution fusion | flops 336593664 | bytes 4458496 | tf_op jit(solution)/shard_map/bme,bmd->bed/dot_general | solution.py:31
  7.4 2.3 copy.216
  10.5 1.2 copy.217
  11.7 69.5 %all_to_all.56 = bf16[4,16,16,1280]{3,0,1,2:T(4,128)(2,1)S(1)} all-to-all(bf16[4,16,16,1280]{3,0,1,2:T(4,128)(2,1)S(1)} %copy.217), channel_id=1, replica_groups=mesh['dp'=16,'expert'=16] {'expert'}, dimensions={2} | all-to-all | bytes 5242880 | tf_op jit(solution)/shard_map/all_to_all | solution.py:38
  81.6 5.7 %fusion.39 = (bf16[64,1,1,1280]{3,1,0,2:T(2,128)(2,1)S(1)}, bf16[64,1,1,1280]{3,1,0,2:T(2,128)(2,1)S(1)}, bf16[64,1,1,1280]{3,1,0,2:T(2,128)(2,1)S(1)}, bf16[64,...) fusion(bf16[64,16,1,1280]{3,1,0,2:T(8,128)(2,1)S(1)} %bitcast.75), kind=kLoop, calls=%fused_computation.55 | loop fusion | bytes 5242880 | tf_op jit(solution)/shard_map/split | solution.py:40
  87.3 0.7 bitcast_dynamic-update-slice_fusion.15
  88.0 0.7 bitcast_dynamic-update-slice_fusion.14
  88.7 0.7 bitcast_dynamic-update-slice_fusion.13
  89.4 0.7 bitcast_dynamic-update-slice_fusion.12
  92.1 0.7 bitcast_dynamic-update-slice_fusion.8
  93.5 0.7 bitcast_dynamic-update-slice_fusion.6
  94.9 0.7 bitcast_dynamic-update-slice_fusion.4
  98.3 10.1 %all-to-all-start.1 = ((bf16[16,64,1,1,1280]{4,1,3,2,0:T(8,128)(2,1)}), bf16[16,64,1,1,1280]{4,1,3,2,0:T(8,128)(2,1)}, u32[]{:S(2)}, u32[]{:S(2)}) async-start(bf16[16,64,1,1,1280]{4,1,3,2,0:T(8,128)(2,1)} %bitcast_dynamic-update-slice_fusion), calls=%async_computation.1 | async-start | bytes 5242880 | tf_op jit(solution)/shard_map/all_to_all | solution.py:40
  108.4 2.1 copy.219
  110.5 5.4 %shift_right_arithmetic.23 = s32[1024,128,10]{0,2,1:T(8,128)} broadcast(s32[1024,128]{0,1:T(8,128)} %copy.219), dimensions={0,1} | broadcast | bytes 5767168 | tf_op jit(solution)/shard_map/shift_right_arithmetic | solution.py:12
  115.9 7.9 %shift_right_arithmetic.24 = s32[1024,1280]{0,1:T(8,128)} reshape(s32[1024,128,10]{0,2,1:T(8,128)} %shift_right_arithmetic.23) | data formatting | bytes 10485760 | tf_op jit(solution)/shard_map/shift_right_arithmetic | solution.py:12
  123.8 5.9 %copy.220 = s32[1024,1280]{1,0:T(8,128)} copy(s32[1024,1280]{0,1:T(8,128)} %shift_right_arithmetic.24) | data formatting | bytes 10485760 | tf_op jit(solution)/shard_map/shift_right_arithmetic | solution.py:12
  129.9 41.3 %all-to-all-done.1 = bf16[16,64,1,1,1280]{4,1,3,2,0:T(8,128)(2,1)} async-done(((bf16[16,64,1,1,1280]{4,1,3,2,0:T(8,128)(2,1)}), bf16[16,64,1,1,1280]{4,1,3,2,0:T(8,128)(2,1)}, u32[]{:S(2)}, u32[]{:S(2)}) %all-to-all-start.1) | async-done | bytes 2621472 | tf_op jit(solution)/shard_map/all_to_all | solution.py:40
  171.2 11.8 %fusion.17 = bf16[1024,1,1,1280]{3,0,2,1:T(8,128)(2,1)} fusion(bf16[1,1280,1280]{2,1,0:T(8,128)(2,1)S(1)} %copy-done, s32[1024,1280]{1,0:T(8,128)} %copy.220, bf16[1024,1280]{1,0:T(8,128)(2,1)} %bitcast.7, bf16[1,1280,1280]{2,1,0:T(8,128)(2,1)} %param.7, s32[1280]{0:T(1024)S(1)} %shift_right_arithmetic.26), kind=kOutput, calls=%fused_computation.18 | convolution fusion | flops 6730547200 | bytes 17044480 | tf_op jit(solution)/shard_map/dot_general | solution.py:19
  183.6 4.5 %reduce.1 = bf16[1024,1280]{1,0:T(8,128)(2,1)S(1)} reduce(bf16[1024,1,1,1280]{3,0,2,1:T(8,128)(2,1)} %fusion.17, bf16[]{:T(256)} %broadcast.8), dimensions={1,2}, to_apply=%copy.221.reduce_sub_computation | reduce | bytes 5242882 | tf_op jit(solution)/shard_map/reshape | solution.py:45
  188.1 2.2 reshape.18
  190.3 57.8 %all_to_all.57 = bf16[16,2,40960]{2,1,0:T(2,128)(2,1)S(1)} all-to-all(bf16[16,2,40960]{2,1,0:T(2,128)(2,1)} %reshape.18), channel_id=1, replica_groups=mesh['dp'=16,'expert'=16] {'dp'}, dimensions={0} | all-to-all | bytes 5242880 | tf_op jit(solution)/shard_map/all_to_all | solution.py:44
  248.1 7.2 %reshape.19 = bf16[1024,1,1,1280]{3,2,1,0:T(2,128)(2,1)} reshape(bf16[16,2,40960]{2,1,0:T(2,128)(2,1)S(1)} %all_to_all.57) | data formatting | bytes 5242880
  255.3 2.9 copy.242
  258.2 2.9 copy.222
  261.1 15.0 %all-to-all-start.3 = ((bf16[64,16,1,1280]{3,1,2,0:T(8,128)(2,1)}), bf16[64,16,1,1280]{3,1,2,0:T(8,128)(2,1)S(1)}, u32[]{:S(2)}, u32[]{:S(2)}) async-start(bf16[64,16,1,1280]{3,1,2,0:T(8,128)(2,1)} %copy.222), calls=%async_computation.3 | async-start | bytes 5242880 | tf_op jit(solution)/shard_map/all_to_all | solution.py:47
  276.5 61.9 %all-to-all-done.3 = bf16[64,16,1,1280]{3,1,2,0:T(8,128)(2,1)S(1)} async-done(((bf16[64,16,1,1280]{3,1,2,0:T(8,128)(2,1)}), bf16[64,16,1,1280]{3,1,2,0:T(8,128)(2,1)S(1)}, u32[]{:S(2)}, u32[]{:S(2)}) %all-to-all-start.3) | async-done | bytes 2621472 | tf_op jit(solution)/shard_map/all_to_all | solution.py:47
  338.3 2.8 copy.223
  341.2 5.1 %reduce_sum.32 = bf16[4,128,1280]{2,0,1:T(4,128)(2,1)} reduce(bf16[4,128,2,1280]{3,0,2,1:T(4,128)(2,1)} %bitcast.77, bf16[]{:T(256)} %constant.8.clone.1), dimensions={2}, to_apply=%region_4.0 | reduce | flops 655360 | bytes 3932162 | tf_op jit(solution)/shard_map/reduce_sum | solution.py:49
  346.3 5.3 %convolution_convert_fusion = bf16[4,256,1280]{2,1,0:T(8,128)(2,1)} fusion(bf16[4,128,1280]{2,0,1:T(4,128)(2,1)} %reduce_sum.32, f32[4,256]{1,0:T(4,128)S(1)} %fusion.41, f32[4,256,128]{2,1,0:T(8,128)} %copy-done.2), kind=kOutput, calls=%fused_computation.13 | convolution fusion | flops 337249408 | bytes 4460544 | tf_op jit(solution)/shard_map/bme,bed->bmd/dot_general | solution.py:50
  (23 shorter events, 8.6 us)
Async XLA Ops:
  0.0 171.2 %copy-start = (bf16[1,1280,1280]{2,1,0:T(8,128)(2,1)S(1)}, bf16[1,1280,1280]{2,1,0:T(8,128)(2,1)}, u32[]{:S(2)}) copy-start(bf16[1,1280,1280]{2,1,0:T(8,128)(2,1)} %param.8) | copy-start | bytes 9830404
  2.8 0.8 copy-start.2
  98.3 72.9 %all-to-all-start.1 = ((bf16[16,64,1,1,1280]{4,1,3,2,0:T(8,128)(2,1)}), bf16[16,64,1,1,1280]{4,1,3,2,0:T(8,128)(2,1)}, u32[]{:S(2)}, u32[]{:S(2)}) async-start(bf16[16,64,1,1,1280]{4,1,3,2,0:T(8,128)(2,1)} %bitcast_dynamic-update-slice_fusion), calls=%async_computation.1 | async-start | bytes 5242880 | tf_op jit(solution)/shard_map/all_to_all | solution.py:40
  261.1 15.0 %copy-start.3 = (f32[4,256,128]{2,1,0:T(8,128)S(1)}, f32[4,256,128]{2,1,0:T(8,128)}, u32[]{:S(2)}) copy-start(f32[4,256,128]{2,1,0:T(8,128)} %copy-done.2) | copy-start | bytes 1572868
  261.1 77.2 %all-to-all-start.3 = ((bf16[64,16,1,1280]{3,1,2,0:T(8,128)(2,1)}), bf16[64,16,1,1280]{3,1,2,0:T(8,128)(2,1)S(1)}, u32[]{:S(2)}, u32[]{:S(2)}) async-start(bf16[64,16,1,1280]{3,1,2,0:T(8,128)(2,1)} %copy.222), calls=%async_computation.3 | async-start | bytes 5242880 | tf_op jit(solution)/shard_map/all_to_all | solution.py:47
  341.2 10.4 %copy-start.1 = (bf16[1,1280,1280]{2,1,0:T(8,128)(2,1)S(1)}, bf16[1,1280,1280]{2,1,0:T(8,128)(2,1)}, u32[]{:S(2)}) copy-start(bf16[1,1280,1280]{2,1,0:T(8,128)(2,1)} %param.8) | copy-start | bytes 9830404
